TPU v7x, 256 devices: a whole 4x4x8 slice. The times are simulated.
256 devices in a mesh: val: 16 (over y_hi, x, core), cond: 16 (over y_lo, z).
Axes of the slice: x: 4, y: 4 (y_hi: 2, y_lo: 2; y = y_hi * 2 + y_lo), z: 8, core: 2. Of those that a mesh axis runs over, the one named last changes fastest.
Arguments:
- trial: bfloat16 [256, 65536], P('val', 'cond'), may hold values from -6 to 6
- pair_cond: bfloat16 [80, 1024, 1024], P('val', 'cond'), may hold values from -0.1875 to 0.1875
- pair_val: bfloat16 [256, 20480], P(None, 'val'), may hold values from -0.0625 to 0.0625
Outputs:
- applied: bfloat16 [256, 65536], P('val', 'cond')
All inputs are finite; a program needn't handle non-finite values.
Results may differ from a plain program's by a relative error of at most 0.0049.
Values may be sent and summed in bfloat16 or wider, within the bound.
A program may use at most 128 MiB of HBM per device.

v0:
```python
import jax
import jax.numpy as jnp
from jax import lax
from jax.sharding import Mesh
from jax.sharding import PartitionSpec as P

S = 64
G = 80
VAL = ("val_0", "val_1", "val_2")


def joined_along(tiles, dim):
    tiles = jnp.moveaxis(tiles, 0, dim)
    lengths = tiles.shape
    return tiles.reshape(*lengths[:dim], lengths[dim] * lengths[dim + 1], *lengths[dim + 2 :])


def from_everyone(x, axis):
    length = lax.axis_size(axis)
    return lax.all_to_all(jnp.broadcast_to(x[None], (length, *x.shape)), axis, 0, 0, tiled=True)


def collect(x, axis, dim):
    return joined_along(from_everyone(x, axis), dim)


def split_up(x, dim, length):
    lengths = x.shape
    tiles = x.reshape(*lengths[:dim], length, lengths[dim] // length, *lengths[dim + 1 :])
    return jnp.moveaxis(tiles, dim, 0)


def sent_and_summed(x, axis, dim):
    tiles = split_up(x, dim, lax.axis_size(axis))
    arrived = lax.all_to_all(tiles, axis, split_axis=0, concat_axis=0, tiled=True)
    return arrived.sum(axis=0)


def sum_in_two_steps(x, axes, dim):
    far, near = axes
    tiles = split_up(x, dim, lax.axis_size(far))
    nearer = sent_and_summed(tiles, near, dim + 1)
    arrived = lax.all_to_all(nearer, far, split_axis=0, concat_axis=0, tiled=True)
    return arrived.sum(axis=0)


def body(trial, pair_cond, pair_val):
    gathered = collect(trial, "cond", 1)
    local_rows = gathered.shape[0]
    whole = gathered.reshape(local_rows, gathered.shape[1] // S, S)
    local_cols = trial.shape[1]
    partner_count = pair_val.shape[1] // G
    val_blocks = pair_val.reshape(pair_val.shape[0], partner_count, G)
    piece = lax.all_gather(pair_cond, VAL, axis=0, tiled=True)
    inner = jnp.einsum("kcd,wds->wkcs", piece, whole, preferred_element_type=jnp.float32)
    inner = inner.reshape(local_rows, piece.shape[0], local_cols).astype(jnp.bfloat16)
    total = jnp.einsum("vwg,wgx->vx", val_blocks, inner, preferred_element_type=jnp.float32)
    result = sum_in_two_steps(total, (("val_0", "val_1"), "val_2"), 0)
    return result.astype(jnp.bfloat16)


def solution(mesh):
    torus = Mesh(
        mesh.devices.reshape(2, 4, 2, mesh.shape["cond"]), ("val_0", "val_1", "val_2", "cond")
    )
    in_specs = (P(VAL, "cond"), P(VAL, "cond", None), P(None, VAL))
    out_specs = P(VAL, "cond")
    return jax.shard_map(body, mesh=torus, in_specs=in_specs, out_specs=out_specs, check_vma=False)
```

profile of v0, /device:TPU:1, one launch (start us, length us, event | category | flops | bytes accessed | tf_op | source)
XLA Modules:
  0.0 214.9 jit_solution(11688042672552102239)
XLA Ops:
  6.5 0.0 copy-start.1
  6.5 0.0 all-gather.2.cloned.1.call-start
  6.5 0.7 all-gather.2.cloned.1.call-update
  7.3 2.5 %broadcast_in_dim.2 = bf16[16,16,4096]{2,1,0:T(8,128)(2,1)} broadcast(bf16[16,4096]{1,0:T(8,128)(2,1)} %param.3), dimensions={1,2} | broadcast | bytes 2228224 | tf_op jit(solution)/shard_map/broadcast_in_dim | solution.py:20
  9.7 10.1 %all-to-all-start = ((bf16[16,16,4096]{2,1,0:T(8,128)(2,1)}), bf16[16,16,4096]{2,1,0:T(8,128)(2,1)S(1)}, u32[]{:S(2)}, u32[]{:S(2)}) async-start(bf16[16,16,4096]{2,1,0:T(8,128)(2,1)} %broadcast_in_dim.2), calls=%async_computation | async-start | bytes 4194304 | tf_op jit(solution)/shard_map/all_to_all | solution.py:20
  19.9 0.0 copy-done.1
  19.9 0.2 copy.20
  20.1 47.4 %all-to-all-done = bf16[16,16,4096]{2,1,0:T(8,128)(2,1)S(1)} async-done(((bf16[16,16,4096]{2,1,0:T(8,128)(2,1)}), bf16[16,16,4096]{2,1,0:T(8,128)(2,1)S(1)}, u32[]{:S(2)}, u32[]{:S(2)}) %all-to-all-start) | async-done | bytes 2097184 | tf_op jit(solution)/shard_map/all_to_all | solution.py:20
  67.5 0.0 copy-start
  67.5 1.3 copy-done
  68.8 2.7 %copy.17 = bf16[16,16,4096]{2,1,0:T(8,128)(2,1)S(1)} copy(bf16[16,16,4096]{2,0,1:T(8,128)(2,1)} %bitcast.26) | data formatting | bytes 4194304 | tf_op jit(solution)/shard_map/transpose | solution.py:13
  71.6 5.5 %reshape_reshape.6 = bf16[16,1024,64]{2,1,0:T(8,128)(2,1)} reshape(bf16[16,16,4096]{2,1,0:T(8,128)(2,1)S(1)} %copy.17) | data formatting | bytes 4194304 | tf_op jit(solution)/shard_map/reshape;reshape | solution.py:50
  77.1 31.5 %all-gather.2.cloned.1.call-done = bf16[80,64,1024]{2,1,0:T(8,128)(2,1)} async-done(((bf16[5,64,1024]{2,1,0:T(8,128)(2,1)}), bf16[80,64,1024]{2,1,0:T(8,128)(2,1)}) %all-gather.2.cloned.1.call-update) | async-done | bytes 10485776 | tf_op jit(solution)/shard_map/all_gather | solution.py:54
  108.6 42.0 %fusion.3 = bf16[16,64,80,64]{2,1,3,0:T(8,128)(2,1)} fusion(bf16[80,64,1024]{2,1,0:T(8,128)(2,1)} %all-gather.2.cloned.1.call-done, bf16[16,1024,64]{2,1,0:T(8,128)(2,1)} %reshape_reshape.6), kind=kOutput, calls=%fused_computation.3 | convolution fusion | flops 10742661120 | bytes 23068672 | tf_op jit(solution)/shard_map/kcd,wds->wkcs/dot_general | solution.py:55
  150.7 10.1 %fusion.7 = f32[4096,256,1]{0,1,2:T(8,128)} fusion(bf16[16,80,4096]{1,2,0:T(8,128)(2,1)} %bitcast.29, bf16[256,16,80]{0,2,1:T(8,128)(2,1)S(1)} %bitcast.28), kind=kOutput, calls=%fused_computation.6 | convolution fusion | flops 2684354560 | bytes 15335424 | tf_op jit(solution)/shard_map/vwg,wgx->vx/dot_general | solution.py:57
  160.8 2.5 %copy.34 = f32[8,2,16,4096]{3,2,0,1:T(8,128)S(1)} copy(f32[8,2,16,4096]{3,2,1,0:T(8,128)} %bitcast.27) | data formatting | bytes 8388608 | tf_op jit(solution)/shard_map/reshape;reshape | solution.py:29
  163.2 8.0 %all_to_all.15 = f32[2,8,16,4096]{3,2,1,0:T(8,128)} all-to-all(f32[2,8,16,4096]{3,2,1,0:T(8,128)S(1)} %bitcast.25), channel_id=1, replica_groups=mesh['val_0'=2,'val_1'=4,'val_2'=2,'cond'=16] {'val_2'}, dimensions={0} | all-to-all | bytes 8388608 | tf_op jit(solution)/shard_map/all_to_all | solution.py:35
  171.3 2.7 %reduce_sum.18 = f32[8,16,4096]{2,1,0:T(8,128)S(1)} reduce(f32[2,8,16,4096]{3,2,1,0:T(8,128)} %all_to_all.15, f32[]{:T(128)} %constant.0.clone.1), dimensions={0}, to_apply=%region_0.0 | reduce | flops 524288 | bytes 6291460 | tf_op jit(solution)/shard_map/reduce_sum | solution.py:36
  174.0 31.7 %all_to_all.16 = f32[8,16,4096]{2,1,0:T(8,128)} all-to-all(f32[8,16,4096]{2,1,0:T(8,128)S(1)} %reduce_sum.18), channel_id=1, replica_groups=mesh['val_0'=2,'val_1'=4,'val_2'=2,'cond'=16] {'val_0','val_1'}, dimensions={0} | all-to-all | bytes 4194304 | tf_op jit(solution)/shard_map/all_to_all | solution.py:43
  205.7 2.4 %reduce_sum.19 = bf16[16,4096]{1,0:T(8,128)(2,1)} reduce(f32[8,16,4096]{2,1,0:T(8,128)} %all_to_all.16, f32[]{:T(128)} %constant.0.clone.1), dimensions={0}, to_apply=%region_1.0 | reduce | flops 458752 | bytes 2228228 | tf_op jit(solution)/shard_map/reduce_sum | solution.py:44
Async XLA Ops:
  6.5 13.3 %copy-start.1 = (bf16[256,1280]{1,0:T(8,128)(2,1)S(1)}, bf16[256,1280]{1,0:T(8,128)(2,1)}, u32[]{:S(2)}) copy-start(bf16[256,1280]{1,0:T(8,128)(2,1)} %param.5) | copy-start | bytes 1966084
  6.5 102.1 %all-gather.2.cloned.1.call-start = ((), (), s32[]{:S(2)}) async-start(), calls=%async_computation.3 | async-start | bytes 11141120 | tf_op jit(solution)/shard_map/all_gather | solution.py:54
  9.7 57.8 %all-to-all-start = ((bf16[16,16,4096]{2,1,0:T(8,128)(2,1)}), bf16[16,16,4096]{2,1,0:T(8,128)(2,1)S(1)}, u32[]{:S(2)}, u32[]{:S(2)}) async-start(bf16[16,16,4096]{2,1,0:T(8,128)(2,1)} %broadcast_in_dim.2), calls=%async_computation | async-start | bytes 4194304 | tf_op jit(solution)/shard_map/all_to_all | solution.py:20
  67.5 1.3 copy-start
Sparse Core Ops, SparseCore 0:
  10.1 98.5 all-gather.1
where the time goes:
time: 215 us
  waiting for transfers between devices  79.6 us (37%)
  matrix products  52.1 us (24%)
  blocking collectives  39.8 us (19%)
  local copies, waits for them, and re-layouts  14.8 us (7%)
  between operations  13.4 us (6%)
  starting transfers between devices  10.1 us (5%)
  other arithmetic  5.07 us (2%)
    all_to_all x1, waiting for transfers between devices, from_everyone(): lax.all_to_all(jnp.broadcast_to(x[None], (length, *x.shape)), axis, 0, 0,...  47.4 us
    dot_general x1, matrix products, body(): jnp.einsum('kcd,wds->wkcs', piece, whole, preferred_element_type=jnp.floa...  42 us
    all_to_all x1, blocking collectives, sum_in_two_steps(): lax.all_to_all(nearer, far, split_axis=0, concat_axis=0, tiled=True)  31.7 us
    all_gather x1, waiting for transfers between devices, body(): piece = lax.all_gather(pair_cond, VAL, axis=0, tiled=True)  31.5 us
    all_to_all x1, starting transfers between devices, from_everyone(): lax.all_to_all(jnp.broadcast_to(x[None], (length, *x.shape)), axis, 0, 0,...  10.1 us
    dot_general x1, matrix products, body(): jnp.einsum('vwg,wgx->vx', val_blocks, inner, preferred_element_type=jnp.f...  10.1 us
    all_to_all x1, blocking collectives, sent_and_summed(): lax.all_to_all(tiles, axis, split_axis=0, concat_axis=0, tiled=True)  8.04 us
    another operation x1, local copies, waits for them, and re-layouts, body(): whole = gathered.reshape(local_rows, gathered.shape[1] // S, S)  5.52 us
  transfers between devices with their start and end apart: 2, of which 2 were waited for; matrix products, arithmetic and copies ran while one was open for 5% of the time, Pallas kernels for 0%

commit v1 on v0

v1 whole, which is shorter than its diff:
```python
import jax
import jax.numpy as jnp
from jax import lax
from jax.experimental import pallas as pl
from jax.experimental.pallas import tpu as pltpu
from jax.sharding import PartitionSpec as P

MESH = pl.DeviceIdType.MESH
F32, BF16 = jnp.float32, jnp.bfloat16
NQ = 4
NJ = 4
Z = 8


def device(x, y, z, core):
    x, y, z = lax.rem(x + 4, 4), lax.rem(y + 4, 4), lax.rem(z + Z, Z)
    return {"val": (y // 2) * 8 + x * 2 + core, "cond": lax.rem(y, 2) * Z + z}


def kernel(trial_ref, pc_hbm, pv_ref, out_ref, pcb, tb, pvs, pvall, perm, bs, ts, ys, xs, acc,
           rbuf, sbuf, obuf, loc_sem, pc_s, pc_r, sib_s, sib_r, ty_s, ty_r, tz_s, tz_r, pv_s, pv_r,
           d2_s, d2_r, o_s, o_r):
    val, cond = lax.axis_index("val"), lax.axis_index("cond")
    yh, yl, z = val // 8, cond // Z, lax.rem(cond, Z)
    x, core, y = lax.rem(val, 8) // 2, lax.rem(val, 2), (val // 8) * 2 + cond // Z
    sibling = device(x, y, z, 1 - core)
    xpeer = [device(x + d, y, z, core) for d in (1, 2, 3)]
    ypeer = [device(x, y + d, z, core) for d in (1, 2, 3)]
    zpeer = [device(x, y, z + 1, core), device(x, y, z - 1, core)]
    opeer = xpeer + [device(x + d, y + 2, z, core) for d in (0, 1, 2, 3)]
    partners = [sibling] + xpeer + ypeer + zpeer + opeer[4:]

    barrier = pltpu.get_barrier_semaphore()
    for p in partners:
        pl.semaphore_signal(barrier, 1, device_id=p, device_id_type=MESH)
    pl.semaphore_wait(barrier, len(partners))

    sent = []

    def send(src, dst, s, r, to):
        cp = pltpu.make_async_remote_copy(src, dst, s, r, device_id=to, device_id_type=MESH)
        cp.start()
        sent.append(cp)
        return cp

    pc_cp, loc_cp = [], []
    for j in range(NJ):
        src = pc_hbm.at[:, pl.ds(j * 16, 16), :]
        cp = pltpu.make_async_copy(src, pcb.at[j, x, core], loc_sem.at[j])
        cp.start()
        loc_cp.append(cp)
        pc_cp.append([send(src, pcb.at[j, x, core], pc_s.at[j, d], pc_r.at[j, d], xpeer[d]) for d in (0, 2, 1)])

    lane = lax.broadcasted_iota(jnp.int32, (32, 128), 1) < 64
    for i in range(32):
        bs[pl.ds(i, 16, stride=32), :] = trial_ref[:, i * 128:(i + 1) * 128].astype(F32)
    ty_cp = []
    for q in range(NQ):
        for half in range(2):
            w = (q * 2 + half) * 2
            b0, b1 = bs[w * 32:w * 32 + 32, :], bs[w * 32 + 32:w * 32 + 64, :]
            ts[pl.ds(0, 32, stride=2), :] = jnp.where(lane, b0, pltpu.roll(b1, 64, 1))
            ts[pl.ds(1, 32, stride=2), :] = jnp.where(lane, pltpu.roll(b0, 64, 1), b1)
            tb[q, yh, yl, z, :, half * 128:half * 128 + 128] = ts[...].astype(BF16)
        mine = tb.at[q, yh, yl, z]
        ty_cp.append([send(mine, mine, ty_s.at[q, d], ty_r.at[q, d], ypeer[d]) for d in (0, 2, 1)])

    def select(h):
        row = lax.broadcasted_iota(jnp.int32, (1280, 640), 0)
        col = lax.broadcasted_iota(jnp.int32, (1280, 640), 1)
        perm[...] = jnp.where(row == col + 40 * ((col * 1639) >> 16) + 40 * h, 1.0, 0.0).astype(BF16)
        return jnp.dot(pv_ref[...], perm[...], preferred_element_type=F32).astype(BF16)

    pvs[...] = select(1 - yh)
    pv_cp = send(pvs, pvall.at[yh], pv_s, pv_r, ypeer[1])
    pvall[yh] = select(yh)

    tz_cp = {}

    def e(q, s):
        if s == 1:
            for cp in ty_cp[q]:
                cp.wait_recv()
        else:
            for cp in tz_cp[q, s - 1]:
                cp.wait_recv()
        near, far = lax.rem(z - (s - 1) + Z, Z), lax.rem(z + s - 1, Z)
        if s < 4:
            a, b = tb.at[q, :, :, near], tb.at[q, :, :, far]
        else:
            a, b = tb.at[q, 0, :, near], tb.at[q, 1, :, far]
        tz_cp[q, s] = [send(a, a, tz_s.at[q, s - 1, 0], tz_r.at[q, s - 1, 0], zpeer[0]),
                       send(b, b, tz_s.at[q, s - 1, 1], tz_r.at[q, s - 1, 1], zpeer[1])]

    def f(q):
        for cp in tz_cp[q, 4]:
            cp.wait_recv()

    sib_cp = {}

    def p(j):
        loc_cp[j].wait()
        for cp in pc_cp[j]:
            cp.wait_recv()
        sib_cp[j] = send(pcb.at[j, :, core], pcb.at[j, :, core], sib_s.at[j], sib_r.at[j], sibling)

    low = lax.broadcasted_iota(jnp.int32, (40, 128), 1) < 64

    def r(q, j):
        if q == 0:
            sib_cp[j].wait_recv()
        lhs = pcb[j].reshape(640, 1024)
        for h in range(2):
            rhs = tb[q, h].reshape(1024, 256)
            prod = jnp.dot(lhs, rhs, preferred_element_type=F32)
            ys[h, 0] = prod[:, :128]
            ys[h, 1] = prod[:, 128:]
            for wp in range(2):
                for cp in range(8):
                    c0 = ys[h, wp, pl.ds(2 * cp, 40, stride=16), :]
                    c1 = ys[h, wp, pl.ds(2 * cp + 1, 40, stride=16), :]
                    w0 = jnp.where(low, c0, pltpu.roll(c1, 64, 1))
                    w1 = jnp.where(low, pltpu.roll(c0, 64, 1), c1)
                    xs[h, wp * 80:wp * 80 + 80, cp * 128:cp * 128 + 128] = jnp.concatenate([w0, w1], 0).astype(BF16)
        total = None
        for h in range(2):
            t = jnp.dot(pvall[h, :, q * 160:q * 160 + 160], xs[h], preferred_element_type=F32)
            total = t if total is None else total + t
        total = total.reshape(8, 2, 16, 1024)
        if q == 0:
            acc[j] = total
        else:
            acc[j] += total

    d2_cp = {}

    def d(j):
        d2_cp[j] = send(acc.at[j, :, 1 - core], rbuf.at[j], d2_s.at[j], d2_r.at[j], sibling)

    o_cp = {}
    who = [lax.rem(x + dx, 4) + 4 * yh for dx in (1, 2, 3)] + [lax.rem(x + dx, 4) + 4 * (1 - yh) for dx in (0, 1, 2, 3)]
    me = x + 4 * yh

    def s(j):
        d2_cp[j].wait_recv()
        sbuf[j] = (acc[j, :, core] + rbuf[j]).astype(BF16)
        o_cp[j] = [send(sbuf.at[j, who[i]], obuf.at[j, i], o_s.at[j, i], o_r.at[j, i], opeer[i]) for i in range(7)]

    def o(j):
        for cp in o_cp[j]:
            cp.wait_recv()
        total = acc[j, me, core] + rbuf[j, me]
        for i in range(7):
            total = total + obuf[j, i].astype(F32)
        out_ref[:, j * 1024:(j + 1) * 1024] = total.astype(BF16)

    e(0, 1)
    e(1, 1)
    e(0, 2)
    e(1, 2)
    p(0)
    e(0, 3)
    e(1, 3)
    e(0, 4)
    e(2, 1)
    e(1, 4)
    p(1)
    f(0)
    e(3, 1)
    f(1)
    pv_cp.wait_recv()
    r(0, 0)
    e(2, 2)
    p(2)
    r(0, 1)
    e(3, 2)
    p(3)
    r(0, 2)
    e(2, 3)
    r(0, 3)
    r(1, 0)
    e(3, 3)
    r(1, 1)
    r(1, 2)
    e(2, 4)
    r(1, 3)
    e(3, 4)
    f(2)
    for j in range(NJ):
        r(2, j)
    f(3)
    for j in range(NJ):
        r(3, j)
        d(j)
        if j:
            s(j - 1)
    s(NJ - 1)
    for j in range(NJ):
        o(j)
    for cp in sent:
        cp.wait_send()


def body(trial, pair_cond, pair_val):
    dma = pltpu.SemaphoreType.DMA
    vmem = pl.BlockSpec(memory_space=pltpu.VMEM)
    return pl.pallas_call(
        kernel,
        out_shape=jax.ShapeDtypeStruct((16, 4096), BF16),
        in_specs=[vmem, pl.BlockSpec(memory_space=pl.ANY), vmem],
        out_specs=vmem,
        scratch_shapes=[
            pltpu.VMEM((NJ, 4, 2, 5, 16, 1024), BF16),
            pltpu.VMEM((NQ, 2, 2, Z, 64, 256), BF16),
            pltpu.VMEM((256, 640), BF16),
            pltpu.VMEM((2, 256, 640), BF16),
            pltpu.VMEM((1280, 640), BF16),
            pltpu.VMEM((512, 128), F32),
            pltpu.VMEM((64, 128), F32),
            pltpu.VMEM((2, 2, 640, 128), F32),
            pltpu.VMEM((2, 160, 1024), BF16),
            pltpu.VMEM((NJ, 8, 2, 16, 1024), F32),
            pltpu.VMEM((NJ, 8, 16, 1024), F32),
            pltpu.VMEM((NJ, 8, 16, 1024), BF16),
            pltpu.VMEM((NJ, 7, 16, 1024), BF16),
            dma((NJ,)), dma((NJ, 3)), dma((NJ, 3)), dma((NJ,)), dma((NJ,)),
            dma((NQ, 3)), dma((NQ, 3)), dma((NQ, 4, 2)), dma((NQ, 4, 2)), dma(()), dma(()),
            dma((NJ,)), dma((NJ,)), dma((NJ, 7)), dma((NJ, 7)),
        ],
        compiler_params=pltpu.CompilerParams(
            collective_id=0, has_side_effects=True, vmem_limit_bytes=56 << 20
        ),
    )(trial, pair_cond, pair_val)


def solution(mesh):
    in_specs = (P("val", "cond"), P("val", "cond", None), P(None, "val"))
    return jax.shard_map(body, mesh=mesh, in_specs=in_specs, out_specs=P("val", "cond"), check_vma=False)
```

time: 215 us -> 86.5 us (0.40)
  Pallas kernels: 0 us -> 84.8 us
  waiting for transfers between devices: 79.6 us -> 0 us
  matrix products: 52.1 us -> 0 us
  blocking collectives: 39.8 us -> 0 us
  between operations: 13.4 us -> 0.01 us
  local copies, waits for them, and re-layouts: 14.8 us -> 1.57 us
  starting transfers between devices: 10.1 us -> 0 us
  other arithmetic: 5.07 us -> 0 us
    pallas_call x0 -> x1, Pallas kernels: none -> 84.8 us  [body(): pl.pallas_call(kernel, out_shape=jax.ShapeDtypeStruct((16, 4096), BF16),...]
    dot_general x2 -> x0, matrix products: 52.1 us -> none  [the longest x1 42 us: body(): jnp.einsum('kcd,wds->wkcs', piece, whole, preferred_element_type=jnp.floa...]
    all_to_all x1 -> x0, waiting for transfers between devices: 47.4 us -> none  [from_everyone(): lax.all_to_all(jnp.broadcast_to(x[None], (length, *x.shape)), axis, 0, 0,...]
    all_to_all x2 -> x0, blocking collectives: 39.8 us -> none  [the longest x1 31.7 us: sum_in_two_steps(): lax.all_to_all(nearer, far, split_axis=0, concat_axis=0, tiled=True)]
    all_gather x1 -> x0, waiting for transfers between devices: 31.5 us -> none  [body(): piece = lax.all_gather(pair_cond, VAL, axis=0, tiled=True)]
    all_to_all x1 -> x0, starting transfers between devices: 10.1 us -> none  [from_everyone(): lax.all_to_all(jnp.broadcast_to(x[None], (length, *x.shape)), axis, 0, 0,...]
    another operation x2 -> x0, local copies, waits for them, and re-layouts: 7.98 us -> none  [the longest x1 5.52 us: body(): whole = gathered.reshape(local_rows, gathered.shape[1] // S, S)]
    reduce_sum x2 -> x0, other arithmetic: 5.07 us -> none  [the longest x1 2.68 us: sent_and_summed(): return arrived.sum(axis=0)]
  transfers between devices with their start and end apart: 2 -> 0, of which waited for: 2 -> 0; matrix products, arithmetic and copies ran while one was open for 5% -> 0% of each run, Pallas kernels for 0% -> 0%
where the time goes in v1:
time: 86.5 us; the launch traced here: 86.4 us
  Pallas kernels  84.8 us (98%)
  local copies, waits for them, and re-layouts  1.57 us (2%)
    pallas_call x1, Pallas kernels, body(): pl.pallas_call(kernel, out_shape=jax.ShapeDtypeStruct((16, 4096), BF16),...  84.8 us

profile of v1, /device:TPU:1, one launch (start us, length us, event | category | flops | bytes accessed | tf_op | source)
XLA Modules:
  0.0 86.4 jit_solution(13857230883550673977)
XLA Ops:
  0.0 84.8 %shard_map.37 = bf16[16,4096]{1,0:T(8,128)(2,1)} custom-call(bf16[16,4096]{1,0:T(8,128)(2,1)} %trial_ref.1, bf16[5,64,1024]{2,1,0:T(8,128)(2,1)} %pc_hbm.1, bf16[256,1280]{1,0:T(8,128)(2,1)} %pv_ref.1), custom_call_target="tpu_custom_call" | custom-call | tf_op jit(solution)/shard_map/pallas_call | solution.py:207
  84.8 1.6 %copy.5 = bf16[16,4096]{1,0:T(8,128)(2,1)} copy(bf16[16,4096]{1,0:T(8,128)(2,1)} %shard_map.37) | data formatting | bytes 262144

commit v2 on v1

--- a/solution.py
+++ b/solution.py
@@ -26,15 +26,13 @@
     sibling = device(x, y, z, 1 - core)
     xpeer = [device(x + d, y, z, core) for d in (1, 2, 3)]
     ypeer = [device(x, y + d, z, core) for d in (1, 2, 3)]
-    zpeer = [device(x, y, z + 1, core), device(x, y, z - 1, core)]
+    zpeer = [device(x, y, z + d, core) for d in (1, -1, 2, -2)]
     opeer = xpeer + [device(x + d, y + 2, z, core) for d in (0, 1, 2, 3)]
     partners = [sibling] + xpeer + ypeer + zpeer + opeer[4:]
 
     barrier = pltpu.get_barrier_semaphore()
     for p in partners:
         pl.semaphore_signal(barrier, 1, device_id=p, device_id_type=MESH)
-    pl.semaphore_wait(barrier, len(partners))
-
     sent = []
 
     def send(src, dst, s, r, to):
@@ -43,18 +41,9 @@
         sent.append(cp)
         return cp
 
-    pc_cp, loc_cp = [], []
-    for j in range(NJ):
-        src = pc_hbm.at[:, pl.ds(j * 16, 16), :]
-        cp = pltpu.make_async_copy(src, pcb.at[j, x, core], loc_sem.at[j])
-        cp.start()
-        loc_cp.append(cp)
-        pc_cp.append([send(src, pcb.at[j, x, core], pc_s.at[j, d], pc_r.at[j, d], xpeer[d]) for d in (0, 2, 1)])
-
     lane = lax.broadcasted_iota(jnp.int32, (32, 128), 1) < 64
     for i in range(32):
         bs[pl.ds(i, 16, stride=32), :] = trial_ref[:, i * 128:(i + 1) * 128].astype(F32)
-    ty_cp = []
     for q in range(NQ):
         for half in range(2):
             w = (q * 2 + half) * 2
@@ -62,8 +51,6 @@
             ts[pl.ds(0, 32, stride=2), :] = jnp.where(lane, b0, pltpu.roll(b1, 64, 1))
             ts[pl.ds(1, 32, stride=2), :] = jnp.where(lane, pltpu.roll(b0, 64, 1), b1)
             tb[q, yh, yl, z, :, half * 128:half * 128 + 128] = ts[...].astype(BF16)
-        mine = tb.at[q, yh, yl, z]
-        ty_cp.append([send(mine, mine, ty_s.at[q, d], ty_r.at[q, d], ypeer[d]) for d in (0, 2, 1)])
 
     def select(h):
         row = lax.broadcasted_iota(jnp.int32, (1280, 640), 0)
@@ -72,10 +59,22 @@
         return jnp.dot(pv_ref[...], perm[...], preferred_element_type=F32).astype(BF16)
 
     pvs[...] = select(1 - yh)
+    pvall[yh] = select(yh)
+
+    pl.semaphore_wait(barrier, len(partners))
+
+    ty_cp, tz_cp, pc_cp, loc_cp = {}, {}, {}, {}
+    both = tb.at[2:4, yh, yl, z]
+    tz_cp[2, 1] = [send(both, both, tz_s.at[2, 0, i], tz_r.at[2, 0, i], zpeer[i]) for i in (0, 1, 2, 3)]
+    for q in range(2):
+        mine = tb.at[q, yh, yl, z]
+        ty_cp[q] = [send(mine, mine, ty_s.at[q, d], ty_r.at[q, d], ypeer[d]) for d in (0, 2, 1)]
+    for j in range(NJ):
+        src = pc_hbm.at[:, pl.ds(j * 16, 16), :]
+        loc_cp[j] = pltpu.make_async_copy(src, pcb.at[j, x, core], loc_sem.at[j])
+        loc_cp[j].start()
+        pc_cp[j] = [send(src, pcb.at[j, x, core], pc_s.at[j, d], pc_r.at[j, d], xpeer[d]) for d in (0, 2)]
     pv_cp = send(pvs, pvall.at[yh], pv_s, pv_r, ypeer[1])
-    pvall[yh] = select(yh)
-
-    tz_cp = {}
 
     def e(q, s):
         if s == 1:
@@ -92,6 +91,34 @@
         tz_cp[q, s] = [send(a, a, tz_s.at[q, s - 1, 0], tz_r.at[q, s - 1, 0], zpeer[0]),
                        send(b, b, tz_s.at[q, s - 1, 1], tz_r.at[q, s - 1, 1], zpeer[1])]
 
+    def a():
+        for cp in tz_cp[2, 1]:
+            cp.wait_recv()
+        near, far = lax.rem(z + Z - 2, Z), lax.rem(z + 2, Z)
+        n3, f3 = tb.at[2:4, yh, yl, near], tb.at[2:4, yh, yl, far]
+        n4, f4 = tb.at[2, yh, yl, near], tb.at[3, yh, yl, far]
+        tz_cp[2, 2] = [send(t, t, tz_s.at[2, 1, i], tz_r.at[2, 1, i], zpeer[i]) for i, t in enumerate((n3, f3, n4, f4))]
+
+    def b(q):
+        if q == 2:
+            for cp in tz_cp[2, 2]:
+                cp.wait_recv()
+        mine = tb.at[q, yh, yl]
+        ty_cp[q] = [send(mine, mine, ty_s.at[q, d], ty_r.at[q, d], ypeer[d]) for d in (0, 2)]
+
+    def c(q):
+        for cp in ty_cp[q]:
+            cp.wait_recv()
+        below, above = lax.rem(y + 3, 4), lax.rem(y + 1, 4)
+        lo = tb.at[q, below // 2, lax.rem(below, 2), 0:4]
+        hi = tb.at[q, above // 2, lax.rem(above, 2), 4:8]
+        ty_cp[q] = [send(lo, lo, ty_s.at[q, 1], ty_r.at[q, 1], ypeer[0]),
+                    send(hi, hi, ty_s.at[q, 3], ty_r.at[q, 3], ypeer[2])]
+
+    def g(q):
+        for cp in ty_cp[q]:
+            cp.wait_recv()
+
     def f(q):
         for cp in tz_cp[q, 4]:
             cp.wait_recv()
@@ -99,38 +126,66 @@
     sib_cp = {}
 
     def p(j):
+        for cp in pc_cp[j]:
+            cp.wait_recv()
+        lo = pcb.at[j, lax.rem(x + 3, 4), core, :, :, 0:512]
+        hi = pcb.at[j, lax.rem(x + 1, 4), core, :, :, 512:1024]
+        pc_cp[j] = [send(lo, lo, pc_s.at[j, 1], pc_r.at[j, 1], xpeer[0]),
+                    send(hi, hi, pc_s.at[j, 3], pc_r.at[j, 3], xpeer[2])]
+
+    def p2(j):
         loc_cp[j].wait()
         for cp in pc_cp[j]:
             cp.wait_recv()
         sib_cp[j] = send(pcb.at[j, :, core], pcb.at[j, :, core], sib_s.at[j], sib_r.at[j], sibling)
 
     low = lax.broadcasted_iota(jnp.int32, (40, 128), 1) < 64
-
-    def r(q, j):
-        if q == 0:
-            sib_cp[j].wait_recv()
-        lhs = pcb[j].reshape(640, 1024)
-        for h in range(2):
-            rhs = tb[q, h].reshape(1024, 256)
-            prod = jnp.dot(lhs, rhs, preferred_element_type=F32)
-            ys[h, 0] = prod[:, :128]
-            ys[h, 1] = prod[:, 128:]
-            for wp in range(2):
-                for cp in range(8):
-                    c0 = ys[h, wp, pl.ds(2 * cp, 40, stride=16), :]
-                    c1 = ys[h, wp, pl.ds(2 * cp + 1, 40, stride=16), :]
-                    w0 = jnp.where(low, c0, pltpu.roll(c1, 64, 1))
-                    w1 = jnp.where(low, pltpu.roll(c0, 64, 1), c1)
-                    xs[h, wp * 80:wp * 80 + 80, cp * 128:cp * 128 + 128] = jnp.concatenate([w0, w1], 0).astype(BF16)
-        total = None
-        for h in range(2):
-            t = jnp.dot(pvall[h, :, q * 160:q * 160 + 160], xs[h], preferred_element_type=F32)
-            total = t if total is None else total + t
-        total = total.reshape(8, 2, 16, 1024)
-        if q == 0:
-            acc[j] = total
+    pend, begun = [], set()
+    parts = [(i, wp, c) for i in range(2) for wp in range(2) for c in range(8)]
+
+    def relay(u, some):
+        pair, h, j, par = u
+        for i, wp, c in some:
+            c0 = ys[par, i, wp, pl.ds(2 * c, 40, stride=16), :]
+            c1 = ys[par, i, wp, pl.ds(2 * c + 1, 40, stride=16), :]
+            w0 = jnp.where(low, c0, pltpu.roll(c1, 64, 1))
+            w1 = jnp.where(low, pltpu.roll(c0, 64, 1), c1)
+            at = i * 160 + wp * 80
+            xs[par, at:at + 80, c * 128:c * 128 + 128] = jnp.concatenate([w0, w1], 0).astype(BF16)
+
+    def finish(u):
+        pair, h, j, par = u
+        t = jnp.dot(pvall[h, :, pair * 320:pair * 320 + 320], xs[par], preferred_element_type=F32)
+        t = t.reshape(8, 2, 16, 1024)
+        if j not in begun:
+            begun.add(j)
+            acc[j] = t
         else:
-            acc[j] += total
+            acc[j] += t
+
+    count = [0]
+
+    def r(pair, h, j):
+        par = count[0] % 2
+        count[0] += 1
+        last = pend.pop() if pend else None
+        for i in range(2):
+            rhs = tb[pair * 2 + i, h].reshape(1024, 256)
+            for m in range(2):
+                prod = jnp.dot(pcb[j, 2 * m:2 * m + 2].reshape(320, 1024), rhs, preferred_element_type=F32)
+                for wp in range(2):
+                    ys[par, i, wp, m * 320:m * 320 + 320] = prod[:, wp * 128:wp * 128 + 128]
+                if last:
+                    at = (i * 2 + m) * 8
+                    relay(last, parts[at:at + 8])
+        if last:
+            finish(last)
+        pend.append((pair, h, j, par))
+
+    def flush():
+        u = pend.pop()
+        relay(u, parts)
+        finish(u)
 
     d2_cp = {}
 
@@ -156,46 +211,47 @@
 
     e(0, 1)
     e(1, 1)
+    a()
     e(0, 2)
+    b(2)
+    b(3)
     e(1, 2)
     p(0)
+    p(1)
     e(0, 3)
+    p(2)
+    p(3)
     e(1, 3)
+    c(2)
+    p2(0)
     e(0, 4)
-    e(2, 1)
+    p2(1)
+    c(3)
     e(1, 4)
-    p(1)
+    p2(2)
+    p2(3)
+    pv_cp.wait_recv()
+    for j in range(NJ):
+        sib_cp[j].wait_recv()
+        r(1, yh, j)
     f(0)
-    e(3, 1)
     f(1)
-    pv_cp.wait_recv()
-    r(0, 0)
-    e(2, 2)
-    p(2)
-    r(0, 1)
-    e(3, 2)
-    p(3)
-    r(0, 2)
-    e(2, 3)
-    r(0, 3)
-    r(1, 0)
-    e(3, 3)
-    r(1, 1)
-    r(1, 2)
-    e(2, 4)
-    r(1, 3)
-    e(3, 4)
-    f(2)
     for j in range(NJ):
-        r(2, j)
-    f(3)
-    for j in range(NJ):
-        r(3, j)
-        d(j)
+        r(0, 0, j)
+        if j:
+            d(j - 1)
+        r(0, 1, j)
+        if j == 0:
+            g(2)
+            g(3)
+        r(1, 1 - yh, j)
         if j:
             s(j - 1)
+    flush()
+    d(NJ - 1)
+    o(0)
     s(NJ - 1)
-    for j in range(NJ):
+    for j in range(1, NJ):
         o(j)
     for cp in sent:
         cp.wait_send()
@@ -217,14 +273,14 @@
             pltpu.VMEM((1280, 640), BF16),
             pltpu.VMEM((512, 128), F32),
             pltpu.VMEM((64, 128), F32),
-            pltpu.VMEM((2, 2, 640, 128), F32),
-            pltpu.VMEM((2, 160, 1024), BF16),
+            pltpu.VMEM((2, 2, 2, 640, 128), F32),
+            pltpu.VMEM((2, 320, 1024), BF16),
             pltpu.VMEM((NJ, 8, 2, 16, 1024), F32),
             pltpu.VMEM((NJ, 8, 16, 1024), F32),
             pltpu.VMEM((NJ, 8, 16, 1024), BF16),
             pltpu.VMEM((NJ, 7, 16, 1024), BF16),
-            dma((NJ,)), dma((NJ, 3)), dma((NJ, 3)), dma((NJ,)), dma((NJ,)),
-            dma((NQ, 3)), dma((NQ, 3)), dma((NQ, 4, 2)), dma((NQ, 4, 2)), dma(()), dma(()),
+            dma((NJ,)), dma((NJ, 4)), dma((NJ, 4)), dma((NJ,)), dma((NJ,)),
+            dma((NQ, 4)), dma((NQ, 4)), dma((NQ, 4, 4)), dma((NQ, 4, 4)), dma(()), dma(()),
             dma((NJ,)), dma((NJ,)), dma((NJ, 7)), dma((NJ, 7)),
         ],
         compiler_params=pltpu.CompilerParams(

time: 86.5 us -> 76.6 us (0.89)
  Pallas kernels: 84.8 us -> 74.9 us
    pallas_call x1, Pallas kernels: 84.8 us -> 74.9 us  [body(): pl.pallas_call(kernel, out_shape=jax.ShapeDtypeStruct((16, 4096), BF16),...]
where the time goes in v2:
time: 76.6 us; the launch traced here: 76.5 us
  Pallas kernels  74.9 us (98%)
  local copies, waits for them, and re-layouts  1.57 us (2%)
    pallas_call x1, Pallas kernels, body(): pl.pallas_call(kernel, out_shape=jax.ShapeDtypeStruct((16, 4096), BF16),...  74.9 us
    unnamed x1, local copies, waits for them, and re-layouts  1.57 us

profile of v2, /device:TPU:1, one launch (start us, length us, event | category | flops | bytes accessed | tf_op | source)
XLA Modules:
  0.0 76.5 jit_solution(4410620781639597503)
XLA Ops:
  0.0 74.9 %shard_map.37 = bf16[16,4096]{1,0:T(8,128)(2,1)} custom-call(bf16[16,4096]{1,0:T(8,128)(2,1)} %trial_ref.1, bf16[5,64,1024]{2,1,0:T(8,128)(2,1)} %pc_hbm.1, bf16[256,1280]{1,0:T(8,128)(2,1)} %pv_ref.1), custom_call_target="tpu_custom_call" | custom-call | tf_op jit(solution)/shard_map/pallas_call | solution.py:263
  74.9 1.6 %copy.5 = bf16[16,4096]{1,0:T(8,128)(2,1)} copy(bf16[16,4096]{1,0:T(8,128)(2,1)} %shard_map.37) | data formatting | bytes 262144

commit v3 on v2

--- a/solution.py
+++ b/solution.py
@@ -17,7 +17,7 @@
     return {"val": (y // 2) * 8 + x * 2 + core, "cond": lax.rem(y, 2) * Z + z}
 
 
-def kernel(trial_ref, pc_hbm, pv_ref, out_ref, pcb, tb, pvs, pvall, perm, bs, ts, ys, xs, acc,
+def kernel(trial_ref, pc_hbm, pv_ref, out_ref, pcb, tb, pvs, pvall, pvc, perm, bs, ts, ys, xs, acc,
            rbuf, sbuf, obuf, loc_sem, pc_s, pc_r, sib_s, sib_r, ty_s, ty_r, tz_s, tz_r, pv_s, pv_r,
            d2_s, d2_r, o_s, o_r):
     val, cond = lax.axis_index("val"), lax.axis_index("cond")
@@ -28,7 +28,7 @@
     ypeer = [device(x, y + d, z, core) for d in (1, 2, 3)]
     zpeer = [device(x, y, z + d, core) for d in (1, -1, 2, -2)]
     opeer = xpeer + [device(x + d, y + 2, z, core) for d in (0, 1, 2, 3)]
-    partners = [sibling] + xpeer + ypeer + zpeer + opeer[4:]
+    partners = [sibling] + xpeer + ypeer + zpeer
 
     barrier = pltpu.get_barrier_semaphore()
     for p in partners:
@@ -55,7 +55,9 @@
     def select(h):
         row = lax.broadcasted_iota(jnp.int32, (1280, 640), 0)
         col = lax.broadcasted_iota(jnp.int32, (1280, 640), 1)
-        perm[...] = jnp.where(row == col + 40 * ((col * 1639) >> 16) + 40 * h, 1.0, 0.0).astype(BF16)
+        wi = (col * 1639) >> 16
+        w = (wi & 12) + ((wi & 1) << 1) + ((wi >> 1) & 1)
+        perm[...] = jnp.where(row == w * 80 + 40 * h + col - 40 * wi, 1.0, 0.0).astype(BF16)
         return jnp.dot(pv_ref[...], perm[...], preferred_element_type=F32).astype(BF16)
 
     pvs[...] = select(1 - yh)
@@ -69,11 +71,14 @@
     for q in range(2):
         mine = tb.at[q, yh, yl, z]
         ty_cp[q] = [send(mine, mine, ty_s.at[q, d], ty_r.at[q, d], ypeer[d]) for d in (0, 2, 1)]
-    for j in range(NJ):
+    def start(j):
         src = pc_hbm.at[:, pl.ds(j * 16, 16), :]
         loc_cp[j] = pltpu.make_async_copy(src, pcb.at[j, x, core], loc_sem.at[j])
         loc_cp[j].start()
-        pc_cp[j] = [send(src, pcb.at[j, x, core], pc_s.at[j, d], pc_r.at[j, d], xpeer[d]) for d in (0, 2)]
+        pc_cp[j] = [send(src, pcb.at[j, x, core], pc_s.at[j, d], pc_r.at[j, d], xpeer[d]) for d in (0, 2, 1)]
+
+    start(0)
+    start(1)
     pv_cp = send(pvs, pvall.at[yh], pv_s, pv_r, ypeer[1])
 
     def e(q, s):
@@ -125,47 +130,37 @@
 
     sib_cp = {}
 
-    def p(j):
-        for cp in pc_cp[j]:
-            cp.wait_recv()
-        lo = pcb.at[j, lax.rem(x + 3, 4), core, :, :, 0:512]
-        hi = pcb.at[j, lax.rem(x + 1, 4), core, :, :, 512:1024]
-        pc_cp[j] = [send(lo, lo, pc_s.at[j, 1], pc_r.at[j, 1], xpeer[0]),
-                    send(hi, hi, pc_s.at[j, 3], pc_r.at[j, 3], xpeer[2])]
-
     def p2(j):
         loc_cp[j].wait()
         for cp in pc_cp[j]:
             cp.wait_recv()
         sib_cp[j] = send(pcb.at[j, :, core], pcb.at[j, :, core], sib_s.at[j], sib_r.at[j], sibling)
 
-    low = lax.broadcasted_iota(jnp.int32, (40, 128), 1) < 64
-    pend, begun = [], set()
-    parts = [(i, wp, c) for i in range(2) for wp in range(2) for c in range(8)]
+    low = lax.broadcasted_iota(jnp.int32, (80, 128), 1) < 64
+    pend = []
+    parts = [(i, c) for i in range(2) for c in range(8)]
 
     def relay(u, some):
-        pair, h, j, par = u
-        for i, wp, c in some:
-            c0 = ys[par, i, wp, pl.ds(2 * c, 40, stride=16), :]
-            c1 = ys[par, i, wp, pl.ds(2 * c + 1, 40, stride=16), :]
-            w0 = jnp.where(low, c0, pltpu.roll(c1, 64, 1))
-            w1 = jnp.where(low, pltpu.roll(c0, 64, 1), c1)
-            at = i * 160 + wp * 80
-            xs[par, at:at + 80, c * 128:c * 128 + 128] = jnp.concatenate([w0, w1], 0).astype(BF16)
+        slot, j, par = u
+        for i, c in some:
+            c0 = jnp.concatenate([ys[par, i, wp, pl.ds(2 * c, 40, stride=16), :] for wp in range(2)], 0).astype(BF16)
+            c1 = jnp.concatenate([ys[par, i, wp, pl.ds(2 * c + 1, 40, stride=16), :] for wp in range(2)], 0).astype(BF16)
+            at = slot * 320 + i * 160
+            xs[at:at + 80, c * 128:c * 128 + 128] = jnp.where(low, c0, pltpu.roll(c1, 64, 1))
+            xs[at + 80:at + 160, c * 128:c * 128 + 128] = jnp.where(low, pltpu.roll(c0, 64, 1), c1)
 
     def finish(u):
-        pair, h, j, par = u
-        t = jnp.dot(pvall[h, :, pair * 320:pair * 320 + 320], xs[par], preferred_element_type=F32)
-        t = t.reshape(8, 2, 16, 1024)
-        if j not in begun:
-            begun.add(j)
-            acc[j] = t
-        else:
-            acc[j] += t
+        slot, j, par = u
+        if slot == 3:
+            t = jnp.dot(pvc[:, 960:1280], xs[960:1280, :], preferred_element_type=F32)
+            acc[j] = t.reshape(8, 2, 16, 1024)
+        elif slot == 2:
+            t = jnp.dot(pvc[:, 0:960], xs[0:960, :], preferred_element_type=F32)
+            acc[j] += t.reshape(8, 2, 16, 1024)
 
     count = [0]
 
-    def r(pair, h, j):
+    def r(slot, pair, h, j):
         par = count[0] % 2
         count[0] += 1
         last = pend.pop() if pend else None
@@ -176,11 +171,11 @@
                 for wp in range(2):
                     ys[par, i, wp, m * 320:m * 320 + 320] = prod[:, wp * 128:wp * 128 + 128]
                 if last:
-                    at = (i * 2 + m) * 8
-                    relay(last, parts[at:at + 8])
+                    at = (i * 2 + m) * 4
+                    relay(last, parts[at:at + 4])
         if last:
             finish(last)
-        pend.append((pair, h, j, par))
+        pend.append((slot, j, par))
 
     def flush():
         u = pend.pop()
@@ -213,38 +208,39 @@
     e(1, 1)
     a()
     e(0, 2)
+    start(2)
     b(2)
     b(3)
     e(1, 2)
-    p(0)
-    p(1)
+    p2(0)
     e(0, 3)
-    p(2)
-    p(3)
+    start(3)
+    p2(1)
     e(1, 3)
     c(2)
-    p2(0)
+    pv_cp.wait_recv()
     e(0, 4)
-    p2(1)
     c(3)
     e(1, 4)
     p2(2)
-    p2(3)
-    pv_cp.wait_recv()
+    for i, (h, at) in enumerate(((0, 0), (1, 0), (1 - yh, 320), (yh, 320))):
+        pvc[:, i * 320:i * 320 + 320] = pvall[h, :, at:at + 320]
     for j in range(NJ):
+        if j == 2:
+            p2(3)
         sib_cp[j].wait_recv()
-        r(1, yh, j)
+        r(3, 1, yh, j)
     f(0)
     f(1)
     for j in range(NJ):
-        r(0, 0, j)
+        r(0, 0, 0, j)
         if j:
             d(j - 1)
-        r(0, 1, j)
+        r(1, 0, 1, j)
         if j == 0:
             g(2)
             g(3)
-        r(1, 1 - yh, j)
+        r(2, 1, 1 - yh, j)
         if j:
             s(j - 1)
     flush()
@@ -270,11 +266,12 @@
             pltpu.VMEM((NQ, 2, 2, Z, 64, 256), BF16),
             pltpu.VMEM((256, 640), BF16),
             pltpu.VMEM((2, 256, 640), BF16),
+            pltpu.VMEM((256, 1280), BF16),
             pltpu.VMEM((1280, 640), BF16),
             pltpu.VMEM((512, 128), F32),
             pltpu.VMEM((64, 128), F32),
             pltpu.VMEM((2, 2, 2, 640, 128), F32),
-            pltpu.VMEM((2, 320, 1024), BF16),
+            pltpu.VMEM((1280, 1024), BF16),
             pltpu.VMEM((NJ, 8, 2, 16, 1024), F32),
             pltpu.VMEM((NJ, 8, 16, 1024), F32),
             pltpu.VMEM((NJ, 8, 16, 1024), BF16),

time: 76.6 us -> 75 us (0.979)
  Pallas kernels: 74.9 us -> 73.4 us
    pallas_call x1, Pallas kernels: 74.9 us -> 73.4 us  [body(): pl.pallas_call(kernel, out_shape=jax.ShapeDtypeStruct((16, 4096), BF16),...]
where the time goes in v3:
time: 75 us; the launch traced here: 74.9 us
  Pallas kernels  73.4 us (98%)
  local copies, waits for them, and re-layouts  1.57 us (2%)
    pallas_call x1, Pallas kernels, body(): pl.pallas_call(kernel, out_shape=jax.ShapeDtypeStruct((16, 4096), BF16),...  73.4 us
    unnamed x1, local copies, waits for them, and re-layouts  1.57 us

profile of v3, /device:TPU:1, one launch (start us, length us, event | category | flops | bytes accessed | tf_op | source)
XLA Modules:
  0.0 74.9 jit_solution(13960112842649875646)
XLA Ops:
  0.0 73.4 %shard_map.37 = bf16[16,4096]{1,0:T(8,128)(2,1)} custom-call(bf16[16,4096]{1,0:T(8,128)(2,1)} %trial_ref.1, bf16[5,64,1024]{2,1,0:T(8,128)(2,1)} %pc_hbm.1, bf16[256,1280]{1,0:T(8,128)(2,1)} %pv_ref.1), custom_call_target="tpu_custom_call" | custom-call | tf_op jit(solution)/shard_map/pallas_call | solution.py:259
  73.4 1.6 %copy.5 = bf16[16,4096]{1,0:T(8,128)(2,1)} copy(bf16[16,4096]{1,0:T(8,128)(2,1)} %shard_map.37) | data formatting | bytes 262144

commit v4 on v3

--- a/solution.py
+++ b/solution.py
@@ -160,19 +160,19 @@
 
     count = [0]
 
-    def r(slot, pair, h, j):
+    def r(slot, pair, h, j, between=None):
         par = count[0] % 2
         count[0] += 1
         last = pend.pop() if pend else None
         for i in range(2):
+            if i and between:
+                between()
             rhs = tb[pair * 2 + i, h].reshape(1024, 256)
-            for m in range(2):
-                prod = jnp.dot(pcb[j, 2 * m:2 * m + 2].reshape(320, 1024), rhs, preferred_element_type=F32)
-                for wp in range(2):
-                    ys[par, i, wp, m * 320:m * 320 + 320] = prod[:, wp * 128:wp * 128 + 128]
-                if last:
-                    at = (i * 2 + m) * 4
-                    relay(last, parts[at:at + 4])
+            if last:
+                relay(last, parts[i * 8:i * 8 + 8])
+            prod = jnp.dot(pcb[j].reshape(640, 1024), rhs, preferred_element_type=F32)
+            for wp in range(2):
+                ys[par, i, wp] = prod[:, wp * 128:wp * 128 + 128]
         if last:
             finish(last)
         pend.append((slot, j, par))
@@ -194,7 +194,7 @@
     def s(j):
         d2_cp[j].wait_recv()
         sbuf[j] = (acc[j, :, core] + rbuf[j]).astype(BF16)
-        o_cp[j] = [send(sbuf.at[j, who[i]], obuf.at[j, i], o_s.at[j, i], o_r.at[j, i], opeer[i]) for i in range(7)]
+        o_cp[j] = [send(sbuf.at[j, who[i]], obuf.at[j, i], o_s.at[j, i], o_r.at[j, i], opeer[i]) for i in (5, 1, 4, 6, 3, 0, 2)]
 
     def o(j):
         for cp in o_cp[j]:
@@ -226,14 +226,13 @@
     for i, (h, at) in enumerate(((0, 0), (1, 0), (1 - yh, 320), (yh, 320))):
         pvc[:, i * 320:i * 320 + 320] = pvall[h, :, at:at + 320]
     for j in range(NJ):
-        if j == 2:
+        if j == 1:
             p2(3)
         sib_cp[j].wait_recv()
         r(3, 1, yh, j)
     f(0)
-    f(1)
     for j in range(NJ):
-        r(0, 0, 0, j)
+        r(0, 0, 0, j, None if j else lambda: f(1))
         if j:
             d(j - 1)
         r(1, 0, 1, j)

time: 75 us -> 74.7 us (level)
  no operation moved by 1% of the time
where the time goes in v4:
time: 74.7 us; the launch traced here: 74.5 us
  Pallas kernels  73 us (98%)
  local copies, waits for them, and re-layouts  1.57 us (2%)
    pallas_call x1, Pallas kernels, body(): pl.pallas_call(kernel, out_shape=jax.ShapeDtypeStruct((16, 4096), BF16),...  73 us
    unnamed x1, local copies, waits for them, and re-layouts  1.57 us

profile of v4, /device:TPU:1, one launch (start us, length us, event | category | flops | bytes accessed | tf_op | source)
XLA Modules:
  0.0 74.5 jit_solution(15334741312452988287)
XLA Ops:
  0.0 73.0 %shard_map.37 = bf16[16,4096]{1,0:T(8,128)(2,1)} custom-call(bf16[16,4096]{1,0:T(8,128)(2,1)} %trial_ref.1, bf16[5,64,1024]{2,1,0:T(8,128)(2,1)} %pc_hbm.1, bf16[256,1280]{1,0:T(8,128)(2,1)} %pv_ref.1), custom_call_target="tpu_custom_call" | custom-call | tf_op jit(solution)/shard_map/pallas_call | solution.py:258
  73.0 1.6 %copy.5 = bf16[16,4096]{1,0:T(8,128)(2,1)} copy(bf16[16,4096]{1,0:T(8,128)(2,1)} %shard_map.37) | data formatting | bytes 262144

commit v5 on v4

--- a/solution.py
+++ b/solution.py
@@ -66,11 +66,11 @@
     pl.semaphore_wait(barrier, len(partners))
 
     ty_cp, tz_cp, pc_cp, loc_cp = {}, {}, {}, {}
-    both = tb.at[2:4, yh, yl, z]
-    tz_cp[2, 1] = [send(both, both, tz_s.at[2, 0, i], tz_r.at[2, 0, i], zpeer[i]) for i in (0, 1, 2, 3)]
     for q in range(2):
         mine = tb.at[q, yh, yl, z]
         ty_cp[q] = [send(mine, mine, ty_s.at[q, d], ty_r.at[q, d], ypeer[d]) for d in (0, 2, 1)]
+    both = tb.at[2:4, yh, yl, z]
+    tz_cp[2, 1] = [send(both, both, tz_s.at[2, 0, i], tz_r.at[2, 0, i], zpeer[i]) for i in (0, 1, 2, 3)]
     def start(j):
         src = pc_hbm.at[:, pl.ds(j * 16, 16), :]
         loc_cp[j] = pltpu.make_async_copy(src, pcb.at[j, x, core], loc_sem.at[j])

time: 74.7 us -> 74.7 us (level)
  no operation moved by 1% of the time
where the time goes in v5:
time: 74.7 us; the launch traced here: 74.5 us
  Pallas kernels  73 us (98%)
  local copies, waits for them, and re-layouts  1.57 us (2%)
    pallas_call x1, Pallas kernels, body(): pl.pallas_call(kernel, out_shape=jax.ShapeDtypeStruct((16, 4096), BF16),...  73 us
    unnamed x1, local copies, waits for them, and re-layouts  1.57 us

profile of v5, /device:TPU:1, one launch (start us, length us, event | category | flops | bytes accessed | tf_op | source)
XLA Modules:
  0.0 74.5 jit_solution(11477910322045892650)
XLA Ops:
  0.0 73.0 %shard_map.37 = bf16[16,4096]{1,0:T(8,128)(2,1)} custom-call(bf16[16,4096]{1,0:T(8,128)(2,1)} %trial_ref.1, bf16[5,64,1024]{2,1,0:T(8,128)(2,1)} %pc_hbm.1, bf16[256,1280]{1,0:T(8,128)(2,1)} %pv_ref.1), custom_call_target="tpu_custom_call" | custom-call | tf_op jit(solution)/shard_map/pallas_call | solution.py:258
  73.0 1.6 %copy.5 = bf16[16,4096]{1,0:T(8,128)(2,1)} copy(bf16[16,4096]{1,0:T(8,128)(2,1)} %shard_map.37) | data formatting | bytes 262144
